TPU v7x, 32 devices: a whole 2x2x4 slice. The times are simulated.
32 devices in a mesh: gx: 16 (over z, y, core), gy: 2 (over x).
Axes of the slice: x: 2, y: 2, z: 4, core: 2. Of those that a mesh axis runs over, the one named last changes fastest.
Arguments:
- loads: float32 [8, 2, 16384], P(None, 'gy', 'gx'), may hold values from -6 to 6
- dual_op: bfloat16 [2, 16384, 1024], P('gy', 'gx')
- iface: int32 [2, 16, 1024], P('gy', 'gx'), may hold values from 0 to 1023, each once within a row
- precond: float32 [2, 16384], P('gy', 'gx'), may hold values from 0.3 to 3
- corner_map: float32 [2, 128, 16384], P('gy', None, 'gx'), may hold values from -0.25 to 0.25
- coarse_inv: float32 [128, 128], replicated
- elem_stiff: float32 [8, 8], replicated
- elem_dofs: int32 [8, 1024, 256], P(None, 'gx', 'gy'), may hold values from 0 to 1023
- density: float32 [1024, 256], P('gx', 'gy'), may hold values from 0.1 to 1
- passive: int32 [1024, 256], P('gx', 'gy'), may hold values 0 or 1
Outputs:
- adjoint: float32 [8, 2, 16384], P(None, 'gy', 'gx')
- sens: float32 [1024, 256], P('gx', 'gy')
All inputs are finite; a program needn't handle non-finite values. No bound on the sum of `passive` on one device may be relied on, other than what follows from the above.
Results may differ from a plain program's by a relative error of at most 0.00052.
Values sent between devices are 32-bit elements; how exact they have to be, the bound alone decides.
No kernel may reach another device: no remote copies, remote signals or barrier semaphores. Data moves between devices by JAX's collectives and lax.ppermute only.
A program may use at most 128 MiB of HBM per device.

v0:
```python
import jax
import jax.numpy as jnp
from jax import lax
from jax.sharding import PartitionSpec as P

R = 128
ITERS = 2
SWEEPS = 3
coupling = 0.3
radius_sq = 2.0
penalty = 3.0


def padded_2(array, sides, width):
    for axis, dim in sides:
        size, length = (lax.axis_size(axis), array.shape[dim])
        up = [(i, (i + 1) % size) for i in range(size - 1)]
        down = [(j, i) for i, j in up]
        last = lax.slice_in_dim(array, length - width, length, axis=dim)
        leading = lax.slice_in_dim(array, 0, width, axis=dim)
        before = lax.ppermute(last, axis, up)
        after = lax.ppermute(leading, axis, down)
        array = jnp.concatenate([before, array, after], axis=dim)
    return array


def local_part(vec, op_local, left_idx, right_idx):
    local = jnp.einsum(
        "ck,mk->cm", vec.astype(jnp.bfloat16), op_local, preferred_element_type=jnp.float32
    )
    width = left_idx.shape[0]
    outgoing = jnp.concatenate([vec[:, left_idx], vec[:, right_idx]], axis=1)
    extended = padded_2(outgoing, (("gx", 1),), width)
    local = local.at[:, left_idx].add(-coupling * extended[:, :width])
    local = local.at[:, right_idx].add(-coupling * extended[:, 3 * width :])
    return local


def apply_dual(vec, op_local, left_idx, right_idx, corners, coarse_inv):
    hi = lax.Precision.HIGHEST
    local = local_part(vec, op_local, left_idx, right_idx)
    csum = lax.psum(jnp.dot(vec, corners.T, precision=hi), ("gx", "gy"))
    coarse_vals = jnp.dot(csum, coarse_inv.T, precision=hi)
    return local + jnp.dot(coarse_vals, corners, precision=hi)


def inner(first, second):
    return jnp.sum(first * second, axis=1)[:, None]


def residual_products(resid, zvec):
    return lax.psum(inner(resid, zvec), ("gx", "gy"))


def on_device(
    loads, dual_op, iface, precond, corner_map, coarse_inv, elem_stiff, elem_dofs, density, passive
):
    hi = lax.Precision.HIGHEST
    op_local = dual_op[0]
    width = R
    left_idx = iface[0, 0, :width]
    right_idx = iface[0, 0, width : 2 * width]
    corners = corner_map[0]
    scaling = precond[0][None, :]
    resid = loads[:, 0, :]
    adjoint = jnp.zeros_like(resid)
    zvec = scaling * resid
    direction = zvec
    rz_now = residual_products(resid, zvec)
    for step in range(ITERS):
        image = apply_dual(direction, op_local, left_idx, right_idx, corners, coarse_inv)
        alpha = rz_now / lax.psum(inner(direction, image), ("gx", "gy"))
        adjoint = adjoint + alpha * direction
        resid = resid - alpha * image
        if step + 1 < ITERS:
            zvec = scaling * resid
            rz_next = residual_products(resid, zvec)
            direction = zvec + rz_next / rz_now * direction
            rz_now = rz_next
    nodal = adjoint[:, elem_dofs]
    pushed = jnp.einsum("ab,cbxy->caxy", elem_stiff, nodal, precision=hi)
    energy = jnp.sum(nodal * pushed, axis=(0, 1))
    grad = jnp.where(passive == 1, 0.0, -penalty * density * density * energy)
    diag = 1.0 + 4.0 * radius_sq
    smooth = grad / diag
    for sweep in range(SWEEPS - 1):
        padded = padded_2(smooth, (("gx", 0), ("gy", 1)), 1)
        beside = padded[2:, 1:-1] + padded[:-2, 1:-1] + padded[1:-1, 2:] + padded[1:-1, :-2]
        smooth = (grad + radius_sq * beside) / diag
    return (adjoint[:, None, :], smooth)


def solution(mesh):
    placed = (
        P(None, "gy", "gx"),
        P("gy", "gx", None),
        P("gy", "gx", None),
        P("gy", "gx"),
        P("gy", None, "gx"),
        P(),
        P(),
        P(None, "gx", "gy"),
        P("gx", "gy"),
        P("gx", "gy"),
    )
    return jax.shard_map(
        on_device,
        mesh=mesh,
        in_specs=placed,
        out_specs=(P(None, "gy", "gx"), P("gx", "gy")),
        check_vma=False,
    )
```

profile of v0, /device:TPU:7, one launch (start us, length us, event | category | flops | bytes accessed | tf_op | source)
XLA Modules:
  0.0 517.5 jit_solution(12681567802003912632)
XLA Ops:
  0.7 0.8 fusion.62
  1.5 1.0 copy.16
  2.5 1.7 bitcast_multiply_fusion.2
  4.2 2.3 gather_fusion
  6.5 3.7 collective-permute-start
  10.2 2.3 gather_fusion.1
  12.5 1.9 collective-permute-start.1
  14.4 0.8 fusion.64
  15.2 0.5 fusion.22
  15.7 39.5 %psum.43 = f32[8,128]{1,0:T(8,128)S(1)} all-reduce(f32[8,128]{1,0:T(8,128)S(1)} %fusion.22), channel_id=1, replica_groups=mesh['gx'=16,'gy'=2] {'gx','gy'}, use_global_device_ids=true, to_apply=%region_2.0 | all-reduce | flops 1024 | bytes 8192 | tf_op jit(solution)/shard_map/psum | solution.py:42
  55.4 0.4 fusion.20
  55.9 0.6 fusion.9
  56.8 1.8 scatter_custom_fusion
  58.6 1.8 scatter_custom_fusion.1
  60.6 41.0 %all-reduce = (f32[8,1]{0,1:T(1,128)S(1)}, f32[8,1]{0,1:T(1,128)S(1)}) all-reduce(f32[8,1]{0,1:T(1,128)S(1)} %bitcast.112, f32[8,1]{0,1:T(1,128)S(1)} %bitcast.111), channel_id=1, replica_groups=mesh['gx'=16,'gy'=2] {'gx','gy'}, use_global_device_ids=true, to_apply=%region_1.0 | all-reduce | flops 16 | bytes 128 | tf_op jit(solution)/shard_map/psum | solution.py:52
  101.8 39.1 %psum.45 = f32[8,1]{0,1:T(1,128)S(1)} all-reduce(f32[8,1]{0,1:T(1,128)S(1)} %bitcast.113), channel_id=1, replica_groups=mesh['gx'=16,'gy'=2] {'gx','gy'}, use_global_device_ids=true, to_apply=%region_8.0 | all-reduce | flops 8 | bytes 64 | tf_op jit(solution)/shard_map/psum | solution.py:52
  141.0 1.2 multiply_add_fusion
  142.3 2.2 fusion.18
  144.4 1.2 gather_fusion.3
  145.7 1.2 gather_fusion.2
  146.9 41.0 %psum.46 = f32[8,128]{1,0:T(8,128)S(1)} all-reduce(f32[8,128]{1,0:T(8,128)S(1)} %fusion.18), channel_id=1, replica_groups=mesh['gx'=16,'gy'=2] {'gx','gy'}, use_global_device_ids=true, to_apply=%region_9.0 | all-reduce | flops 1024 | bytes 8192 | tf_op jit(solution)/shard_map/psum | solution.py:42
  188.1 1.5 fusion.16
  189.5 4.1 collective-permute-start.2
  193.6 1.9 collective-permute-start.3
  195.6 0.6 fusion.12
  196.2 1.0 copy.18
  197.2 3.3 scatter_custom_fusion.2
  200.6 3.1 scatter_custom_fusion.3
  203.7 1.2 multiply_reduce_fusion
  204.9 38.9 %psum.47 = f32[8,1]{0,1:T(1,128)S(1)} all-reduce(f32[8,1]{0,1:T(1,128)S(1)} %bitcast.114), channel_id=1, replica_groups=mesh['gx'=16,'gy'=2] {'gx','gy'}, use_global_device_ids=true, to_apply=%region_13.0 | all-reduce | flops 8 | bytes 64 | tf_op jit(solution)/shard_map/psum | solution.py:72
  243.8 1.2 multiply_add_fusion.1
  245.1 215.5 %gather_fusion.4 = f32[65536,8]{1,0:T(8,128)} fusion(f32[8,1024]{0,1:T(8,128)S(1)} %multiply_add_fusion.1, s32[65536]{0:T(1024)S(1)} %broadcast_clamp_fusion), kind=kCustom, calls=%fused_computation.4 | custom fusion | bytes 4456448 | tf_op jit(solution)/shard_map/gather | solution.py:80
  460.6 18.7 %copy.20 = f32[8,64,128,8]{2,0,1,3:T(8,128)} copy(f32[8,64,128,8]{3,2,1,0:T(8,128)} %bitcast.103) | data formatting | bytes 4194304 | tf_op jit(solution)/shard_map/gather | solution.py:80
  479.2 4.2 fusion
  483.5 5.7 %collective-permute-start.5 = (f32[1,128]{1,0:T(1,128)S(1)}, f32[1,128]{1,0:T(1,128)S(1)}, u32[]{:S(2)}, u32[]{:S(2)}) collective-permute-start(f32[1,128]{1,0:T(1,128)S(1)} %get-tuple-element.20), channel_id=1, source_target_pairs={{0,2},{2,4},{4,6},{6,8},{8,10},{10,12},{12,14},{14,16},{16,18},{18... | collective-permute-start | bytes 1544 | tf_op jit(solution)/shard_map/ppermute | solution.py:21
  489.2 1.9 collective-permute-start.4
  491.2 3.8 collective-permute-done.4
  495.1 1.4 collective-permute-start.6
  496.5 1.3 collective-permute-start.7
  497.8 3.4 collective-permute-done.7
  501.3 3.6 collective-permute-start.9
  504.9 1.9 collective-permute-start.8
  506.9 3.8 collective-permute-done.8
  510.8 1.3 collective-permute-start.10
  512.1 1.3 collective-permute-start.11
  513.4 0.8 copy.21
  514.2 2.6 collective-permute-done.11
  516.8 0.7 fusion.43
  (56 shorter events, 1.5 us)
Async XLA Ops:
  0.6 55.3 %copy-start = (bf16[1,1024,1024]{2,1,0:T(8,128)(2,1)S(1)}, bf16[1,1024,1024]{2,1,0:T(8,128)(2,1)}, u32[]{:S(2)}) copy-start(bf16[1,1024,1024]{2,1,0:T(8,128)(2,1)} %param.11) | copy-start | bytes 6291460
  0.6 14.6 %copy-start.2 = (f32[1,128,1024]{2,1,0:T(8,128)S(1)}, f32[1,128,1024]{2,1,0:T(8,128)}, u32[]{:S(2)}) copy-start(f32[1,128,1024]{2,1,0:T(8,128)} %param.14) | copy-start | bytes 1572868
  0.7 54.6 %copy-start.4 = (f32[128,128]{1,0:T(8,128)S(1)}, f32[128,128]{1,0:T(8,128)}, u32[]{:S(2)}) copy-start(f32[128,128]{1,0:T(8,128)} %param.15) | copy-start | bytes 196612
  0.7 55.1 %copy-start.5 = (s32[8,64,128]{2,1,0:T(8,128)S(1)}, s32[8,64,128]{2,1,0:T(8,128)}, u32[]{:S(2)}) copy-start(s32[8,64,128]{2,1,0:T(8,128)} %param.17) | copy-start | bytes 786436
  1.5 13.7 %copy-start.11 = (s32[128]{0:T(128)}, s32[128]{0:T(128)S(1)}, u32[]{:S(2)}) copy-start(s32[128]{0:T(128)S(1)} %get-tuple-element.23) | copy-start | bytes 1540
  1.5 57.1 %copy-start.10 = (s32[128]{0:T(128)}, s32[128]{0:T(128)S(1)}, u32[]{:S(2)}) copy-start(s32[128]{0:T(128)S(1)} %get-tuple-element.22) | copy-start | bytes 1540
  6.5 50.3 %collective-permute-start = (f32[8,128]{0,1:T(8,128)}, f32[8,128]{0,1:T(8,128)}, u32[]{:S(2)}, u32[]{:S(2)}) collective-permute-start(f32[8,128]{0,1:T(8,128)} %bitcast.9), channel_id=1, source_target_pairs={{0,2},{2,4},{4,6},{6,8},{8,10},{10,12},{12,14},{14,16},{16,18},{18... | collective-permute-start | bytes 12296 | tf_op jit(solution)/shard_map/ppermute | solution.py:21
  12.5 46.1 %collective-permute-start.1 = (f32[8,128]{0,1:T(8,128)}, f32[8,128]{0,1:T(8,128)}, u32[]{:S(2)}, u32[]{:S(2)}) collective-permute-start(f32[8,128]{0,1:T(8,128)} %bitcast.11), channel_id=1, source_target_pairs={{2,0},{4,2},{6,4},{8,6},{10,8},{12,10},{14,12},{16,14},{18,16},{20... | collective-permute-start | bytes 12296 | tf_op jit(solution)/shard_map/ppermute | solution.py:22
  55.8 4.5 copy-start.6
  60.4 80.6 %copy-start.3 = (f32[8,1024]{0,1:T(8,128)}, f32[8,1024]{0,1:T(8,128)S(1)}, u32[]{:S(2)}) copy-start(f32[8,1024]{0,1:T(8,128)S(1)} %scatter_custom_fusion.1) | copy-start | bytes 98308
  141.0 4.7 copy-start.12
  142.3 61.4 %copy-start.1 = (f32[8,1024]{0,1:T(8,128)}, f32[8,1024]{0,1:T(8,128)S(1)}, u32[]{:S(2)}) copy-start(f32[8,1024]{0,1:T(8,128)S(1)} %multiply_add_fusion) | copy-start | bytes 98308
  189.5 7.7 %collective-permute-start.2 = (f32[8,128]{0,1:T(8,128)}, f32[8,128]{0,1:T(8,128)}, u32[]{:S(2)}, u32[]{:S(2)}) collective-permute-start(f32[8,128]{0,1:T(8,128)} %bitcast.116), channel_id=1, source_target_pairs={{0,2},{2,4},{4,6},{6,8},{8,10},{10,12},{12,14},{14,16},{16,18},{18... | collective-permute-start | bytes 12296 | tf_op jit(solution)/shard_map/ppermute | solution.py:21
  193.6 50.2 %copy-start.13 = (f32[8,1]{0,1:T(1,128)S(1)}, f32[8,1]{0,1:T(1,128)}, u32[]{:S(2)}) copy-start(f32[8,1]{0,1:T(1,128)} %copy-done.12) | copy-start | bytes 100
  193.6 6.9 %collective-permute-start.3 = (f32[8,128]{0,1:T(8,128)}, f32[8,128]{0,1:T(8,128)S(1)}, u32[]{:S(2)}, u32[]{:S(2)}) collective-permute-start(f32[8,128]{0,1:T(8,128)} %bitcast.115), channel_id=1, source_target_pairs={{2,0},{4,2},{6,4},{8,6},{10,8},{12,10},{14,12},{16,14},{18,16},{20... | collective-permute-start | bytes 12296 | tf_op jit(solution)/shard_map/ppermute | solution.py:22
  460.6 18.7 %copy-start.9 = (f32[8,8]{1,0:T(8,128)S(1)}, f32[8,8]{1,0:T(8,128)}, u32[]{:S(2)}) copy-start(f32[8,8]{1,0:T(8,128)} %param.16) | copy-start | bytes 772
  479.2 4.3 copy-start.7
  479.2 4.3 copy-start.8
  483.5 7.6 %collective-permute-start.5 = (f32[1,128]{1,0:T(1,128)S(1)}, f32[1,128]{1,0:T(1,128)S(1)}, u32[]{:S(2)}, u32[]{:S(2)}) collective-permute-start(f32[1,128]{1,0:T(1,128)S(1)} %get-tuple-element.20), channel_id=1, source_target_pairs={{0,2},{2,4},{4,6},{6,8},{8,10},{10,12},{12,14},{14,16},{16,18},{18... | collective-permute-start | bytes 1544 | tf_op jit(solution)/shard_map/ppermute | solution.py:21
  489.2 5.8 %collective-permute-start.4 = (f32[1,128]{1,0:T(1,128)S(1)}, f32[1,128]{1,0:T(1,128)S(1)}, u32[]{:S(2)}, u32[]{:S(2)}) collective-permute-start(f32[1,128]{1,0:T(1,128)S(1)} %get-tuple-element.21), channel_id=1, source_target_pairs={{2,0},{4,2},{6,4},{8,6},{10,8},{12,10},{14,12},{16,14},{18,16},{20... | collective-permute-start | bytes 1544 | tf_op jit(solution)/shard_map/ppermute | solution.py:22
  495.1 2.7 collective-permute-start.6
  496.5 4.7 collective-permute-start.7
  501.3 5.6 %collective-permute-start.9 = (f32[1,128]{1,0:T(1,128)S(1)}, f32[1,128]{1,0:T(1,128)S(1)}, u32[]{:S(2)}, u32[]{:S(2)}) collective-permute-start(f32[1,128]{1,0:T(1,128)S(1)} %get-tuple-element.18), channel_id=1, source_target_pairs={{0,2},{2,4},{4,6},{6,8},{8,10},{10,12},{12,14},{14,16},{16,18},{18... | collective-permute-start | bytes 1544 | tf_op jit(solution)/shard_map/ppermute | solution.py:21
  504.9 5.8 %collective-permute-start.8 = (f32[1,128]{1,0:T(1,128)S(1)}, f32[1,128]{1,0:T(1,128)S(1)}, u32[]{:S(2)}, u32[]{:S(2)}) collective-permute-start(f32[1,128]{1,0:T(1,128)S(1)} %get-tuple-element.19), channel_id=1, source_target_pairs={{2,0},{4,2},{6,4},{8,6},{10,8},{12,10},{14,12},{16,14},{18,16},{20... | collective-permute-start | bytes 1544 | tf_op jit(solution)/shard_map/ppermute | solution.py:22
  510.8 3.4 collective-permute-start.10
  512.1 4.7 collective-permute-start.11
where the time goes:
time: 519 us; the launch traced here: 517 us
  local copies, waits for them, and re-layouts  244 us (47%)
  blocking collectives  200 us (39%)
  starting transfers between devices  30 us (6%)
  other arithmetic  18.4 us (4%)
  waiting for transfers between devices  13.7 us (3%)
  matrix products  10.4 us (2%)
    gather x2, local copies, waits for them, and re-layouts, on_device(): nodal = adjoint[:, elem_dofs]  234 us
    psum x2, blocking collectives, apply_dual(): csum = lax.psum(jnp.dot(vec, corners.T, precision=hi), ('gx', 'gy'))  80.5 us
    psum x2, blocking collectives, residual_products(): return lax.psum(inner(resid, zvec), ('gx', 'gy'))  80.2 us
    psum x1, blocking collectives, on_device(): alpha = rz_now / lax.psum(inner(direction, image), ('gx', 'gy'))  38.9 us
    ppermute x6, starting transfers between devices, padded_2(): before = lax.ppermute(last, axis, up)  19.7 us
  transfers between devices with their start and end apart: 12, of which 4 were waited for; matrix products, arithmetic and copies ran while one was open for 2% of the time, Pallas kernels for 0%

commit v1 on v0

--- a/solution.py
+++ b/solution.py
@@ -69,7 +69,7 @@
     rz_now = residual_products(resid, zvec)
     for step in range(ITERS):
         image = apply_dual(direction, op_local, left_idx, right_idx, corners, coarse_inv)
-        alpha = rz_now / lax.psum(inner(direction, image), ("gx", "gy"))
+        alpha = rz_now / lax.psum(lax.psum(inner(direction, image), "gy"), "gx")
         adjoint = adjoint + alpha * direction
         resid = resid - alpha * image
         if step + 1 < ITERS:

time: 519 us -> 542 us (1.044)
  blocking collectives: 200 us -> 220 us
    psum x1 -> x4, blocking collectives: 38.9 us -> 58.9 us  [on_device(): alpha = rz_now / lax.psum(lax.psum(inner(direction, image), 'gy'), 'gx')]
where the time goes in v1:
time: 542 us; the launch traced here: 539 us
  local copies, waits for them, and re-layouts  243 us (45%)
  blocking collectives  220 us (41%)
  starting transfers between devices  31.8 us (6%)
  other arithmetic  19.7 us (4%)
  waiting for transfers between devices  13 us (2%)
  matrix products  10.4 us (2%)
    gather x2, local copies, waits for them, and re-layouts, on_device(): nodal = adjoint[:, elem_dofs]  234 us
    psum x2, blocking collectives, residual_products(): return lax.psum(inner(resid, zvec), ('gx', 'gy'))  82.7 us
    psum x2, blocking collectives, apply_dual(): csum = lax.psum(jnp.dot(vec, corners.T, precision=hi), ('gx', 'gy'))  78.6 us
    psum x4, blocking collectives, on_device(): alpha = rz_now / lax.psum(lax.psum(inner(direction, image), 'gy'), 'gx')  58.9 us
    ppermute x6, starting transfers between devices, padded_2(): before = lax.ppermute(last, axis, up)  20.5 us
    ppermute x6, starting transfers between devices, padded_2(): after = lax.ppermute(leading, axis, down)  11.3 us
  transfers between devices with their start and end apart: 12, of which 4 were waited for; matrix products, arithmetic and copies ran while one was open for 2% of the time, Pallas kernels for 0%

profile of v1, /device:TPU:7, one launch (start us, length us, event | category | flops | bytes accessed | tf_op | source)
XLA Modules:
  0.0 539.3 jit_solution(11949246691706915664)
XLA Ops:
  0.7 0.8 fusion.62
  1.5 1.0 copy.16
  2.5 1.7 bitcast_multiply_fusion.2
  4.2 2.3 gather_fusion
  6.4 3.7 collective-permute-start
  10.1 2.3 gather_fusion.1
  12.4 1.9 collective-permute-start.1
  14.3 0.8 fusion.64
  15.7 39.5 %psum.57 = f32[8,128]{1,0:T(8,128)S(1)} all-reduce(f32[8,128]{1,0:T(8,128)S(1)} %fusion.22), channel_id=1, replica_groups=mesh['gx'=16,'gy'=2] {'gx','gy'}, use_global_device_ids=true, to_apply=%region_2.0 | all-reduce | flops 1024 | bytes 8192 | tf_op jit(solution)/shard_map/psum | solution.py:42
  56.6 1.8 scatter_custom_fusion
  58.4 1.8 scatter_custom_fusion.1
  60.5 3.8 psum.58
  64.3 0.7 compare_select_fusion
  65.0 28.0 %psum.59 = f32[8,1]{0,1:T(1,128)S(1)} all-reduce(f32[8,1]{0,1:T(1,128)S(1)} %psum.58), channel_id=1, replica_groups=mesh['gx'=16,'gy'=2] {'gx'}, use_global_device_ids=true, to_apply=%region_7.0 | all-reduce | flops 8 | bytes 64 | tf_op jit(solution)/shard_map/psum | solution.py:72
  93.0 40.9 %psum.56 = f32[8,1]{0,1:T(1,128)S(1)} all-reduce(f32[8,1]{0,1:T(1,128)S(1)} %bitcast.111), channel_id=1, replica_groups=mesh['gx'=16,'gy'=2] {'gx','gy'}, use_global_device_ids=true, to_apply=%region_1.0 | all-reduce | flops 8 | bytes 64 | tf_op jit(solution)/shard_map/psum | solution.py:52
  134.1 41.8 %psum.60 = f32[8,1]{0,1:T(1,128)S(1)} all-reduce(f32[8,1]{0,1:T(1,128)S(1)} %bitcast.113), channel_id=1, replica_groups=mesh['gx'=16,'gy'=2] {'gx','gy'}, use_global_device_ids=true, to_apply=%region_9.0 | all-reduce | flops 8 | bytes 64 | tf_op jit(solution)/shard_map/psum | solution.py:52
  175.9 1.2 multiply_add_fusion
  177.2 2.2 fusion.18
  179.3 0.7 gather_fusion.3
  180.6 39.1 %psum.61 = f32[8,128]{1,0:T(8,128)S(1)} all-reduce(f32[8,128]{1,0:T(8,128)S(1)} %fusion.18), channel_id=1, replica_groups=mesh['gx'=16,'gy'=2] {'gx','gy'}, use_global_device_ids=true, to_apply=%region_10.0 | all-reduce | flops 1024 | bytes 8192 | tf_op jit(solution)/shard_map/psum | solution.py:42
  219.9 1.5 fusion.16
  221.3 6.0 %collective-permute-start.2 = (f32[8,128]{0,1:T(8,128)S(1)}, f32[8,128]{0,1:T(8,128)S(1)}, u32[]{:S(2)}, u32[]{:S(2)}) collective-permute-start(f32[8,128]{0,1:T(8,128)S(1)} %bitcast.116), channel_id=1, source_target_pairs={{0,2},{2,4},{4,6},{6,8},{8,10},{10,12},{12,14},{14,16},{16,18},{18... | collective-permute-start | bytes 12296 | tf_op jit(solution)/shard_map/ppermute | solution.py:21
  227.3 1.9 collective-permute-start.3
  229.9 1.0 copy.18
  230.9 3.1 scatter_custom_fusion.2
  234.1 3.0 scatter_custom_fusion.3
  237.1 1.2 multiply_reduce_fusion
  238.3 4.0 psum.62
  242.3 1.0 broadcast_clamp_fusion
  243.3 23.1 %psum.63 = f32[8,1]{0,1:T(1,128)S(1)} all-reduce(f32[8,1]{0,1:T(1,128)S(1)} %psum.62), channel_id=1, replica_groups=mesh['gx'=16,'gy'=2] {'gx'}, use_global_device_ids=true, to_apply=%region_15.0 | all-reduce | flops 8 | bytes 64 | tf_op jit(solution)/shard_map/psum | solution.py:72
  266.4 1.2 multiply_add_fusion.1
  267.7 215.5 %gather_fusion.4 = f32[65536,8]{1,0:T(8,128)} fusion(f32[8,1024]{0,1:T(8,128)S(1)} %multiply_add_fusion.1, s32[65536]{0:T(1024)S(1)} %broadcast_clamp_fusion), kind=kCustom, calls=%fused_computation.4 | custom fusion | bytes 4456448 | tf_op jit(solution)/shard_map/gather | solution.py:80
  483.2 18.7 %copy.20 = f32[8,64,128,8]{2,0,1,3:T(8,128)} copy(f32[8,64,128,8]{3,2,1,0:T(8,128)} %bitcast.103) | data formatting | bytes 4194304 | tf_op jit(solution)/shard_map/gather | solution.py:80
  501.8 4.2 fusion
  506.1 4.8 collective-permute-start.5
  511.0 1.9 collective-permute-start.4
  512.9 3.8 collective-permute-done.4
  516.8 1.6 collective-permute-start.6
  518.4 1.3 collective-permute-start.7
  519.7 3.4 collective-permute-done.7
  523.3 3.4 collective-permute-start.9
  526.7 2.6 collective-permute-start.8
  529.3 3.1 collective-permute-done.8
  532.5 1.3 collective-permute-start.10
  533.9 1.3 collective-permute-start.11
  535.2 0.8 copy.21
  535.9 2.6 collective-permute-done.11
  538.6 0.7 fusion.43
  (53 shorter events, 4.2 us)
Async XLA Ops:
  0.6 55.1 %copy-start = (bf16[1,1024,1024]{2,1,0:T(8,128)(2,1)S(1)}, bf16[1,1024,1024]{2,1,0:T(8,128)(2,1)}, u32[]{:S(2)}) copy-start(bf16[1,1024,1024]{2,1,0:T(8,128)(2,1)} %param.11) | copy-start | bytes 6291460
  0.6 14.5 %copy-start.2 = (f32[1,128,1024]{2,1,0:T(8,128)S(1)}, f32[1,128,1024]{2,1,0:T(8,128)}, u32[]{:S(2)}) copy-start(f32[1,128,1024]{2,1,0:T(8,128)} %param.14) | copy-start | bytes 1572868
  0.7 54.5 %copy-start.4 = (f32[128,128]{1,0:T(8,128)S(1)}, f32[128,128]{1,0:T(8,128)}, u32[]{:S(2)}) copy-start(f32[128,128]{1,0:T(8,128)} %param.15) | copy-start | bytes 196612
  1.5 13.6 %copy-start.10 = (s32[128]{0:T(128)}, s32[128]{0:T(128)S(1)}, u32[]{:S(2)}) copy-start(s32[128]{0:T(128)S(1)} %get-tuple-element.21) | copy-start | bytes 1540
  6.4 50.2 %collective-permute-start = (f32[8,128]{0,1:T(8,128)}, f32[8,128]{0,1:T(8,128)}, u32[]{:S(2)}, u32[]{:S(2)}) collective-permute-start(f32[8,128]{0,1:T(8,128)} %bitcast.9), channel_id=1, source_target_pairs={{0,2},{2,4},{4,6},{6,8},{8,10},{10,12},{12,14},{14,16},{16,18},{18... | collective-permute-start | bytes 12296 | tf_op jit(solution)/shard_map/ppermute | solution.py:21
  12.4 46.0 %collective-permute-start.1 = (f32[8,128]{0,1:T(8,128)}, f32[8,128]{0,1:T(8,128)}, u32[]{:S(2)}, u32[]{:S(2)}) collective-permute-start(f32[8,128]{0,1:T(8,128)} %bitcast.11), channel_id=1, source_target_pairs={{2,0},{4,2},{6,4},{8,6},{10,8},{12,10},{14,12},{16,14},{18,16},{20... | collective-permute-start | bytes 12296 | tf_op jit(solution)/shard_map/ppermute | solution.py:22
  55.8 4.5 copy-start.6
  55.8 8.5 %copy-start.5 = (s32[8,64,128]{2,1,0:T(8,128)S(1)}, s32[8,64,128]{2,1,0:T(8,128)}, u32[]{:S(2)}) copy-start(s32[8,64,128]{2,1,0:T(8,128)} %param.17) | copy-start | bytes 786436
  60.2 115.7 %copy-start.3 = (f32[8,1024]{0,1:T(8,128)}, f32[8,1024]{0,1:T(8,128)S(1)}, u32[]{:S(2)}) copy-start(f32[8,1024]{0,1:T(8,128)S(1)} %scatter_custom_fusion.1) | copy-start | bytes 98308
  177.1 59.9 %copy-start.1 = (f32[8,1024]{0,1:T(8,128)}, f32[8,1024]{0,1:T(8,128)S(1)}, u32[]{:S(2)}) copy-start(f32[8,1024]{0,1:T(8,128)S(1)} %multiply_add_fusion) | copy-start | bytes 98308
  221.3 9.6 %collective-permute-start.2 = (f32[8,128]{0,1:T(8,128)S(1)}, f32[8,128]{0,1:T(8,128)S(1)}, u32[]{:S(2)}, u32[]{:S(2)}) collective-permute-start(f32[8,128]{0,1:T(8,128)S(1)} %bitcast.116), channel_id=1, source_target_pairs={{0,2},{2,4},{4,6},{6,8},{8,10},{10,12},{12,14},{14,16},{16,18},{18... | collective-permute-start | bytes 12296 | tf_op jit(solution)/shard_map/ppermute | solution.py:21
  227.3 6.7 %collective-permute-start.3 = (f32[8,128]{0,1:T(8,128)S(1)}, f32[8,128]{0,1:T(8,128)S(1)}, u32[]{:S(2)}, u32[]{:S(2)}) collective-permute-start(f32[8,128]{0,1:T(8,128)S(1)} %bitcast.115), channel_id=1, source_target_pairs={{2,0},{4,2},{6,4},{8,6},{10,8},{12,10},{14,12},{16,14},{18,16},{20... | collective-permute-start | bytes 12296 | tf_op jit(solution)/shard_map/ppermute | solution.py:22
  483.2 18.7 %copy-start.9 = (f32[8,8]{1,0:T(8,128)S(1)}, f32[8,8]{1,0:T(8,128)}, u32[]{:S(2)}) copy-start(f32[8,8]{1,0:T(8,128)} %param.16) | copy-start | bytes 772
  501.8 4.3 copy-start.7
  501.8 4.3 copy-start.8
  506.1 6.8 %collective-permute-start.5 = (f32[1,128]{1,0:T(1,128)S(1)}, f32[1,128]{1,0:T(1,128)S(1)}, u32[]{:S(2)}, u32[]{:S(2)}) collective-permute-start(f32[1,128]{1,0:T(1,128)S(1)} %get-tuple-element.18), channel_id=1, source_target_pairs={{0,2},{2,4},{4,6},{6,8},{8,10},{10,12},{12,14},{14,16},{16,18},{18... | collective-permute-start | bytes 1544 | tf_op jit(solution)/shard_map/ppermute | solution.py:21
  511.0 5.8 %collective-permute-start.4 = (f32[1,128]{1,0:T(1,128)S(1)}, f32[1,128]{1,0:T(1,128)S(1)}, u32[]{:S(2)}, u32[]{:S(2)}) collective-permute-start(f32[1,128]{1,0:T(1,128)S(1)} %get-tuple-element.19), channel_id=1, source_target_pairs={{2,0},{4,2},{6,4},{8,6},{10,8},{12,10},{14,12},{16,14},{18,16},{20... | collective-permute-start | bytes 1544 | tf_op jit(solution)/shard_map/ppermute | solution.py:22
  516.8 2.9 collective-permute-start.6
  518.4 4.7 collective-permute-start.7
  523.3 6.1 %collective-permute-start.9 = (f32[1,128]{1,0:T(1,128)S(1)}, f32[1,128]{1,0:T(1,128)S(1)}, u32[]{:S(2)}, u32[]{:S(2)}) collective-permute-start(f32[1,128]{1,0:T(1,128)S(1)} %get-tuple-element.16), channel_id=1, source_target_pairs={{0,2},{2,4},{4,6},{6,8},{8,10},{10,12},{12,14},{14,16},{16,18},{18... | collective-permute-start | bytes 1544 | tf_op jit(solution)/shard_map/ppermute | solution.py:21
  526.7 5.8 %collective-permute-start.8 = (f32[1,128]{1,0:T(1,128)S(1)}, f32[1,128]{1,0:T(1,128)S(1)}, u32[]{:S(2)}, u32[]{:S(2)}) collective-permute-start(f32[1,128]{1,0:T(1,128)S(1)} %get-tuple-element.17), channel_id=1, source_target_pairs={{2,0},{4,2},{6,4},{8,6},{10,8},{12,10},{14,12},{16,14},{18,16},{20... | collective-permute-start | bytes 1544 | tf_op jit(solution)/shard_map/ppermute | solution.py:22
  532.5 3.4 collective-permute-start.10
  533.9 4.7 collective-permute-start.11
